TPU v7x, 512 devices: a whole 4x8x8 slice. The times are simulated.
512 devices in a mesh: rep: 4 (over y_hi, core), sp: 128 (over y_lo, z, x).
Axes of the slice: x: 4, y: 8 (y_hi: 2, y_lo: 4; y = y_hi * 4 + y_lo), z: 8, core: 2. Of those that a mesh axis runs over, the one named last changes fastest.
Arguments:
- film_start: float32 [4, 2048, 2048], P('rep', 'sp'), may hold values from 0.2 to 2
- evaporation: float32 [4, 2048, 2048], P('rep', 'sp'), may hold values from 0.05 to 0.5
- contact_mask: int32 [4, 2048, 2048], P('rep', 'sp'), may hold values 0 or 1
- first_classes: int32 [4, 2048, 16], P('rep'), may hold values from 0 to 3
- second_classes: int32 [4, 2048, 16], P('rep', 'sp'), may hold values from 0 to 3
- span_inverses: float32 [4, 128, 128], replicated, may hold values from -0.4 to 1
- conv_weight: bfloat16 [3, 3, 4, 64], replicated, may hold values from -0.5 to 0.5
- mixing_weight: bfloat16 [64, 64], replicated, may hold values from -0.75 to 0.75
- flux_weight: bfloat16 [64], replicated, may hold values from -0.75 to 0.75
- film_cotangent: float32 [4, 2048, 2048], P('rep', 'sp'), may hold values from -6 to 6
Outputs:
- final_film: float32 [4, 2048, 2048], P('rep', 'sp')
- film_grad: float32 [4, 2048, 2048], P('rep', 'sp')
- conv_grad: float32 [3, 3, 4, 64], replicated
- mixing_grad: float32 [64, 64], replicated
- flux_grad: float32 [64], replicated
All inputs are finite; a program needn't handle non-finite values. No bound on the sum of `contact_mask` on one device may be relied on, other than what follows from the above.
Results may differ from a plain program's by a relative error of at most 0.019.
Values may be sent and summed in bfloat16 or wider, within the bound.
A program may use at most 128 MiB of HBM per device.

v0:
```python
from functools import partial
import math
import jax
import jax.numpy as jnp
from jax import lax
from jax.sharding import PartitionSpec as P

STEPS = 1
time_step = 0.5


def extended(array, sides, width):
    for axis, dim in sides:
        size, length = (lax.axis_size(axis), array.shape[dim])
        up = [(i, (i + 1) % size) for i in range(size - 1)]
        down = [(j, i) for i, j in up]
        last = lax.slice_in_dim(array, length - width, length, axis=dim)
        first = lax.slice_in_dim(array, 0, width, axis=dim)
        before = lax.ppermute(last, axis, up)
        after = lax.ppermute(first, axis, down)
        array = jnp.concatenate([before, array, after], axis=dim)
    return array


def select_product(tile_rows, matrix, hits, current):
    product = jnp.dot(tile_rows, matrix, precision=lax.Precision.HIGHEST)
    return jnp.where(hits[:, None], product, current)


def keep_same(current):
    return current


def apply_spans(vectors, classes, inverses, transpose):
    count = vectors.shape[0]
    tile_size = math.gcd(128, count)
    line_order = jnp.argsort(classes, stable=True)
    ordered = jnp.take(vectors, line_order, axis=0)
    ordered_cls = jnp.take(classes, line_order)
    results = []
    for start in range(0, count, tile_size):
        tile_rows = ordered[start : start + tile_size]
        tile_cls = ordered_cls[start : start + tile_size]
        result = jnp.zeros_like(tile_rows)
        for group in range(inverses.shape[0]):
            matrix = inverses[group] if transpose else inverses[group].T
            hits = tile_cls == group
            result = lax.cond(
                jnp.any(hits), partial(select_product, tile_rows, matrix, hits), keep_same, result
            )
        results.append(result)
    joined = jnp.concatenate(results, axis=0)
    return jnp.zeros_like(vectors).at[line_order].set(joined)


def solve_lines(lines, classes, inverses, transpose):
    span = inverses.shape[1]
    vectors = lines.reshape(-1, span)
    return apply_spans(vectors, classes.reshape(-1), inverses, transpose).reshape(lines.shape)


def relayout(field):
    moved = lax.all_to_all(field, "sp", split_axis=2, concat_axis=1, tiled=True)
    return jnp.swapaxes(moved, 1, 2)


def split_columns(padded, width):
    count = (padded.shape[-1] - 2) // width
    return jnp.stack(
        [padded[..., number * width : number * width + width + 2] for number in range(count)]
    )


def join_blocks(blocks):
    moved = jnp.moveaxis(blocks, 0, -2)
    return moved.reshape(moved.shape[:-2] + (moved.shape[-2] * moved.shape[-1],))


def cut_blocks(field, width):
    shape = field.shape
    reshaped = field.reshape(shape[:-1] + (shape[-1] // width, width))
    return jnp.moveaxis(reshaped, -2, 0)


def join_padded(blocks):
    middle = jnp.moveaxis(blocks[..., 1:-1], 0, -2)
    left = jnp.moveaxis(blocks[..., 0], 0, -1)
    right = jnp.moveaxis(blocks[..., -1], 0, -1)
    middle = middle.at[..., :-1, -1].add(left[..., 1:])
    middle = middle.at[..., 1:, 0].add(right[..., :-1])
    return middle.reshape(middle.shape[:-2] + (middle.shape[-2] * middle.shape[-1],))


def tap_stack(piece):
    rows = piece.shape[2] - 2
    cols = piece.shape[3] - 2
    return jnp.concatenate(
        [
            piece[:, :, row_tap : row_tap + rows, col_tap : col_tap + cols]
            for row_tap in range(3)
            for col_tap in range(3)
        ],
        axis=0,
    )


def closure_forward(piece, conv_w, mixing_w, flux_w):
    stacked = tap_stack(piece)
    conv_matrix = conv_w.reshape(-1, conv_w.shape[-1])
    first_tanh = jnp.tanh(
        jnp.einsum("ko,krxy->orxy", conv_matrix, stacked, preferred_element_type=jnp.float32)
    )
    first_act = first_tanh.astype(jnp.bfloat16)
    second_tanh = jnp.tanh(
        jnp.einsum("op,orxy->prxy", mixing_w, first_act, preferred_element_type=jnp.float32)
    )
    second_act = second_tanh.astype(jnp.bfloat16)
    flux = jnp.einsum("p,prxy->rxy", flux_w, second_act, preferred_element_type=jnp.float32)
    return (flux, first_tanh, first_act, second_tanh, second_act, stacked)


def closure_backward(piece, flux_cot, conv_w, mixing_w, flux_w):
    rows = piece.shape[2] - 2
    cols = piece.shape[3] - 2
    channels = piece.shape[0]
    flux, first_tanh, first_act, second_tanh, second_act, stacked = closure_forward(
        piece, conv_w, mixing_w, flux_w
    )
    flux_part = jnp.einsum("prxy,rxy->p", second_act, flux_cot, preferred_element_type=jnp.float32)
    second_cot = (flux_w.astype(jnp.float32)[:, None, None, None] * flux_cot[None]).astype(
        jnp.bfloat16
    )
    pre_second_cot = second_cot * (1.0 - second_tanh * second_tanh)
    mixing_part = jnp.einsum(
        "orxy,prxy->op", first_act, pre_second_cot, preferred_element_type=jnp.float32
    )
    first_cot = jnp.einsum(
        "op,prxy->orxy", mixing_w, pre_second_cot, preferred_element_type=jnp.float32
    ).astype(jnp.bfloat16)
    pre_first_cot = first_cot * (1.0 - first_tanh * first_tanh)
    conv_part = jnp.einsum(
        "orxy,krxy->ko", pre_first_cot, stacked, preferred_element_type=jnp.float32
    ).reshape(conv_w.shape)
    conv_matrix = conv_w.reshape(-1, conv_w.shape[-1])
    tap_cots = jnp.einsum(
        "ko,orxy->krxy", conv_matrix, pre_first_cot, preferred_element_type=jnp.float32
    )
    piece_cot = jnp.zeros(piece.shape, jnp.float32)
    for row_tap in range(3):
        for col_tap in range(3):
            number = row_tap * 3 + col_tap
            term = tap_cots[number * channels : (number + 1) * channels]
            piece_cot = piece_cot.at[:, :, row_tap : row_tap + rows, col_tap : col_tap + cols].add(
                term
            )
    edges = jnp.stack([pre_first_cot[:, :, 0], pre_first_cot[:, :, -1]], axis=2)
    return (piece_cot, conv_part, mixing_part, flux_part, edges)


def rim_terms(neighbour, conv_w, row_tap, cols):
    padded = jnp.pad(neighbour, ((0, 0), (0, 0), (1, 1)))
    total = None
    for col_tap in range(3):
        term = jnp.einsum(
            "co,ory->cry",
            conv_w[row_tap, col_tap],
            padded[:, :, 2 - col_tap : 2 - col_tap + cols],
            preferred_element_type=jnp.float32,
        )
        total = term if total is None else total + term
    return total


def on_device(
    film_start,
    evaporation,
    contact_mask,
    first_classes,
    second_classes,
    span_inverses,
    conv_weight,
    mixing_weight,
    flux_weight,
    film_cotangent,
):
    maskf = contact_mask.astype(jnp.float32)
    side = film_start.shape[2]
    side_dev = film_start.shape[1]
    nspan = first_classes.shape[2]
    sp_index = lax.axis_index("sp")
    block_width = min(512, side)

    def first_solve(field, transpose):
        own_first = lax.dynamic_slice(
            first_classes, (0, sp_index * side_dev, 0), (1, side_dev, nspan)
        )
        solved = solve_lines(relayout(field), own_first, span_inverses, transpose)
        return relayout(solved)

    def forward_block(piece):
        return closure_forward(piece, conv_weight, mixing_weight, flux_weight)[0]

    def backward_block(items):
        return closure_backward(items[0], items[1], conv_weight, mixing_weight, flux_weight)

    height = film_start
    step = 0
    features = jnp.stack([height, height * height, maskf, evaporation]).astype(jnp.bfloat16)
    rimmed = extended(features, (("sp", 2),), 1)
    padded = jnp.pad(rimmed, ((0, 0), (0, 0), (0, 0), (1, 1)))
    pieces = split_columns(padded, block_width)
    flux = join_blocks(lax.map(forward_block, pieces))
    source_side = height + time_step * (flux - maskf * evaporation)
    across = first_solve(source_side, False)
    saved = [(height, pieces)]
    height = solve_lines(across, second_classes, span_inverses, False)
    final_film = height
    grad = film_cotangent
    conv_total = jnp.zeros(conv_weight.shape, jnp.float32)
    mixing_total = jnp.zeros(mixing_weight.shape, jnp.float32)
    flux_total = jnp.zeros(flux_weight.shape, jnp.float32)
    for step in reversed(range(STEPS)):
        height, pieces = saved[step]
        back = solve_lines(grad, second_classes, span_inverses, True)
        source_grad = first_solve(back, True)
        flux_cot = cut_blocks(time_step * source_grad, block_width)
        piece_cots, conv_parts, mixing_parts, flux_parts, edges = lax.map(
            backward_block, (pieces, flux_cot)
        )
        conv_total = jnp.sum(conv_parts, axis=0)
        mixing_total = jnp.sum(mixing_parts, axis=0)
        flux_total = jnp.sum(flux_parts, axis=0)
        whole = join_padded(piece_cots)
        inner = whole[:, :, 1:-1]
        rims = extended(join_blocks(edges).astype(jnp.bfloat16), (("sp", 2),), 1).astype(
            jnp.float32
        )
        inner = inner.at[:, :, 0].add(rim_terms(rims[:, :, 0], conv_weight, 2, side))
        inner = inner.at[:, :, -1].add(rim_terms(rims[:, :, 3], conv_weight, 0, side))
        feature_cot = inner.astype(jnp.bfloat16)
        grad = source_grad + feature_cot[0] + 2.0 * height * feature_cot[1]
    conv_sum, mixing_sum, flux_sum = lax.psum((conv_total, mixing_total, flux_total), ("rep", "sp"))
    scale = 1.0 / math.sqrt(lax.axis_size("rep") * film_start.shape[0] * side * side)
    return (final_film, grad, conv_sum * scale, mixing_sum * scale, flux_sum * scale)


def solution(mesh):
    return jax.shard_map(
        on_device,
        mesh=mesh,
        in_specs=(
            P("rep", "sp", None),
            P("rep", "sp", None),
            P("rep", "sp", None),
            P("rep", None, None),
            P("rep", "sp", None),
            P(),
            P(),
            P(),
            P(),
            P("rep", "sp", None),
        ),
        out_specs=(P("rep", "sp", None), P("rep", "sp", None), P(), P(), P()),
        check_vma=False,
    )
```

profile of v0, /device:TPU:2, one launch (start us, length us, event | category | flops | bytes accessed | tf_op | source)
XLA Modules:
  0.0 486.8 jit_solution(13716353377885899539)
XLA Ops:
  6.4 5.7 %collective-permute-start.1 = (bf16[4,1,1,2048]{3,2,1,0:T(2,128)(2,1)S(1)}, bf16[4,1,1,2048]{3,2,1,0:T(2,128)(2,1)S(1)}, u32[]{:S(2)}, u32[]{:S(2)}) collective-permute-start(bf16[4,1,1,2048]{3,2,1,0:T(2,128)(2,1)S(1)} %get-tuple-element.1389), channel_id=1, source_target_pairs={{1,0},{2,1},{3,2},{4,3},{5,4},{6,5},{7,6},{8,7},{9,8},{10,9},{11,1... | collective-permute-start | bytes 49160 | tf_op jit(solution)/shard_map/ppermute | solution.py:20
  35.1 9.3 %reduce.65 = f32[2048,16]{1,0:T(8,128)S(1)} reduce(f32[2048,1,16]{2,1,0:T(1,128)S(1)} %bitcast.494, f32[]{:T(128)} %broadcast.556), dimensions={1}, to_apply=%bitcast.318.reduce_sub_computation | reduce | bytes 262148
  45.5 15.7 %all-to-all-start.2 = ((f32[128,1,256]{2,1,0:T(1,128)}), f32[128,1,256]{2,1,0:T(1,128)S(1)}, u32[]{:S(2)}, u32[]{:S(2)}) async-start(f32[128,1,256]{2,1,0:T(1,128)} %reshape.1187), calls=%async_computation.2 | async-start | bytes 262144 | tf_op jit(solution)/shard_map/all_to_all | solution.py:63
  83.1 9.3 %reduce.67 = f32[2048,16]{1,0:T(8,128)S(1)} reduce(f32[2048,1,16]{2,1,0:T(1,128)S(1)} %bitcast.495, f32[]{:T(128)} %broadcast.556), dimensions={1}, to_apply=%bitcast.320.reduce_sub_computation | reduce | bytes 262148
  93.5 13.1 %all-to-all-start.3 = ((f32[128,1,256]{2,1,0:T(1,128)}), f32[128,1,256]{2,1,0:T(1,128)S(1)}, u32[]{:S(2)}, u32[]{:S(2)}) async-start(f32[128,1,256]{2,1,0:T(1,128)} %reshape.1189), calls=%async_computation.3 | async-start | bytes 262144 | tf_op jit(solution)/shard_map/all_to_all | solution.py:63
  106.6 7.4 %while.44 = (s32[]{:T(128)}, f32[4,1,16,512]{3,2,1,0:T(8,128)S(1)}, bf16[4,4,1,18,514]{4,1,3,2,0:T(4,128)(2,1)S(1)}, bf16[3,3,4,64]{3,2,1,0:T(4,128)(2,1)S(1)}, ...) while((s32[]{:T(128)}, f32[4,1,16,512]{3,2,1,0:T(8,128)S(1)}, ...), condition=%wide.region_11.13_spmd, body=%wide.region_10.12_spmd.sunk | while | flops 106954752 | bytes 5314845 | solution.py:212
  124.8 156.3 %while.45 = (s32[]{:T(128)}, f32[4,4,1,18,514]{4,1,3,2,0:T(4,128)}, f32[4,3,3,4,64]{4,3,2,1,0:T(4,128)}, f32[4,64,64]{2,1,0:T(8,128)}, f32[4,64]{1,0:T(4,128)}, ...) while((s32[]{:T(128)}, f32[4,4,1,18,514]{4,1,3,2,0:T(4,128)}, ...), condition=%wide.region_90.93_spmd, body=%wide.region_88.92_spmd.sunk | while | flops 327188544 | bytes 51537856 | solution.py:227
  141.4 4.0 scatter-add.90
  147.5 4.0 scatter-add.91
  180.5 4.0 scatter-add.90
  186.5 4.0 scatter-add.91
  219.5 4.0 scatter-add.90
  225.5 4.0 scatter-add.91
  258.5 4.0 scatter-add.90
  264.5 4.0 scatter-add.91
  281.1 4.8 copy.228
  286.5 5.3 %fusion.141 = (f32[4,4,1,18,512]{3,1,0,4,2:T(4,128)S(1)}, f32[4,1,18,4,512]{2,0,3,4,1:T(4,128)}) fusion(f32[4,4,1,18,514]{3,1,0,4,2:T(4,128)} %copy.228), kind=kLoop, calls=%fused_computation.279 | loop fusion | bytes 1769472 | tf_op jit(solution)/shard_map/slice | solution.py:86
  302.9 4.3 copy.231
  310.5 9.3 %reduce.69 = f32[2048,16]{1,0:T(8,128)S(1)} reduce(f32[2048,1,16]{2,1,0:T(1,128)S(1)} %bitcast.496, f32[]{:T(128)} %broadcast.556), dimensions={1}, to_apply=%bitcast.314.reduce_sub_computation | reduce | bytes 262148
  320.9 13.3 %all-to-all-start = ((f32[128,1,256]{2,1,0:T(1,128)}), f32[128,1,256]{2,1,0:T(1,128)S(1)}, u32[]{:S(2)}, u32[]{:S(2)}) async-start(f32[128,1,256]{2,1,0:T(1,128)} %reshape.1183), calls=%async_computation | async-start | bytes 262144 | tf_op jit(solution)/shard_map/all_to_all | solution.py:63
  334.4 97.6 %all-reduce.4 = (f32[3,3,4,64]{3,2,1,0:T(4,128)S(1)}, f32[64,64]{1,0:T(8,128)S(1)}, f32[64]{0:T(128)S(1)}) all-reduce(f32[3,3,4,64]{3,2,1,0:T(4,128)S(1)} %reduce_sum.27, f32[64,64]{1,0:T(8,128)S(1)} %reduce_sum.28, f32[64]{0:T(128)S(1)} %reduce_sum.29), channel_id=1, replica_groups=mesh['rep'=4,'sp'=128] {'rep','sp'}, use_global_device_ids=true, to_apply=%region_93.96 | all-reduce | flops 6464 | bytes 51712 | tf_op jit(solution)/shard_map/psum | solution.py:242
  442.9 9.3 %reduce.71 = f32[2048,16]{1,0:T(8,128)S(1)} reduce(f32[2048,1,16]{2,1,0:T(1,128)S(1)} %bitcast.497, f32[]{:T(128)} %broadcast.556), dimensions={1}, to_apply=%bitcast.316.reduce_sub_computation | reduce | bytes 262148
  453.2 9.4 %all-to-all-start.1 = ((f32[128,1,256]{2,1,0:T(1,128)}), f32[128,1,256]{2,1,0:T(1,128)S(1)}, u32[]{:S(2)}, u32[]{:S(2)}) async-start(f32[128,1,256]{2,1,0:T(1,128)} %reshape.1185), calls=%async_computation.1 | async-start | bytes 262144 | tf_op jit(solution)/shard_map/all_to_all | solution.py:63
  464.5 10.1 %all-to-all-done.1 = f32[128,1,256]{2,1,0:T(1,128)S(1)} async-done(((f32[128,1,256]{2,1,0:T(1,128)}), f32[128,1,256]{2,1,0:T(1,128)S(1)}, u32[]{:S(2)}, u32[]{:S(2)}) %all-to-all-start.1) | async-done | bytes 131104 | tf_op jit(solution)/shard_map/all_to_all | solution.py:63
  (547 shorter events, 232.7 us)
Async XLA Ops:
  0.6 27.3 %copy-start.22 = (f32[1,16,2048]{2,1,0:T(8,128)S(1)}, f32[1,16,2048]{2,1,0:T(8,128)}, u32[]{:S(2)}) copy-start(f32[1,16,2048]{2,1,0:T(8,128)} %param.117) | copy-start | bytes 393220
  1.7 27.1 %copy-start.20 = (f32[4,128,128]{2,1,0:T(8,128)S(1)}, f32[4,128,128]{2,1,0:T(8,128)}, u32[]{:S(2)}) copy-start(f32[4,128,128]{2,1,0:T(8,128)} %param.113) | copy-start | bytes 786436
  3.0 67.6 %collective-permute-start = (bf16[4,1,1,2048]{3,2,1,0:T(2,128)(2,1)S(1)}, bf16[4,1,1,2048]{3,2,1,0:T(2,128)(2,1)S(1)}, u32[]{:S(2)}, u32[]{:S(2)}) collective-permute-start(bf16[4,1,1,2048]{3,2,1,0:T(2,128)(2,1)S(1)} %get-tuple-element.1388), channel_id=1, source_target_pairs={{0,1},{1,2},{2,3},{3,4},{4,5},{5,6},{6,7},{7,8},{8,9},{9,10},{10,1... | collective-permute-start | bytes 49160 | tf_op jit(solution)/shard_map/ppermute | solution.py:19
  6.4 64.2 %collective-permute-start.1 = (bf16[4,1,1,2048]{3,2,1,0:T(2,128)(2,1)S(1)}, bf16[4,1,1,2048]{3,2,1,0:T(2,128)(2,1)S(1)}, u32[]{:S(2)}, u32[]{:S(2)}) collective-permute-start(bf16[4,1,1,2048]{3,2,1,0:T(2,128)(2,1)S(1)} %get-tuple-element.1389), channel_id=1, source_target_pairs={{1,0},{2,1},{3,2},{4,3},{5,4},{6,5},{7,6},{8,7},{9,8},{10,9},{11,1... | collective-permute-start | bytes 49160 | tf_op jit(solution)/shard_map/ppermute | solution.py:20
  19.4 61.3 %copy-start.60 = (s32[256]{0:T(256)}, s32[256]{0:T(256)S(1)}, u32[]{:S(2)}) copy-start(s32[256]{0:T(256)S(1)} %get-tuple-element.1420) | copy-start | bytes 3076
  35.1 28.9 %copy-start.62 = (s32[5]{0:T(128)S(1)}, s32[5]{0:T(128)}, u32[]{:S(2)}) copy-start(s32[5]{0:T(128)} %constant.563.clone.1) | copy-start | bytes 64
  35.1 35.3 %copy-start.5 = (bf16[64,64]{1,0:T(8,128)(2,1)S(1)}, bf16[64,64]{1,0:T(8,128)(2,1)}, u32[]{:S(2)}) copy-start(bf16[64,64]{1,0:T(8,128)(2,1)} %param.115) | copy-start | bytes 24580
  45.5 27.5 %all-to-all-start.2 = ((f32[128,1,256]{2,1,0:T(1,128)}), f32[128,1,256]{2,1,0:T(1,128)S(1)}, u32[]{:S(2)}, u32[]{:S(2)}) async-start(f32[128,1,256]{2,1,0:T(1,128)} %reshape.1187), calls=%async_computation.2 | async-start | bytes 262144 | tf_op jit(solution)/shard_map/all_to_all | solution.py:63
  61.2 17.3 %copy-start.32 = (s32[1024]{0:T(1024)}, s32[1024]{0:T(1024)S(1)}, u32[]{:S(2)}) copy-start(s32[1024]{0:T(1024)S(1)} %pad_clamp_fusion) | copy-start | bytes 12292
  64.0 16.7 %copy-start.41 = (pred[128]{0:T(512)(128)(4,1)}, pred[128]{0:T(512)(128)(4,1)S(1)}, u32[]{:S(2)}) copy-start(pred[128]{0:T(512)(128)(4,1)S(1)} %get-tuple-element.1409) | copy-start | bytes 388
  82.5 24.1 %copy-start.12 = (bf16[3,3,4,64]{3,2,1,0:T(4,128)(2,1)S(1)}, bf16[3,3,4,64]{3,2,1,0:T(4,128)(2,1)}, u32[]{:S(2)}) copy-start(bf16[3,3,4,64]{3,2,1,0:T(4,128)(2,1)} %param.114) | copy-start | bytes 13828
  82.5 24.1 %copy-start.26 = (bf16[64]{0:T(256)(128)(2,1)S(1)}, bf16[64]{0:T(256)(128)(2,1)}, u32[]{:S(2)}) copy-start(bf16[64]{0:T(256)(128)(2,1)} %param.116) | copy-start | bytes 388
  83.1 23.5 %copy-start.23 = (f32[4,1,16,512]{3,2,1,0:T(8,128)S(1)}, f32[4,1,16,512]{3,2,1,0:T(8,128)}, u32[]{:S(2)}) copy-start(f32[4,1,16,512]{3,2,1,0:T(8,128)} %custom-call.12) | copy-start | bytes 393220
  93.5 24.9 %all-to-all-start.3 = ((f32[128,1,256]{2,1,0:T(1,128)}), f32[128,1,256]{2,1,0:T(1,128)S(1)}, u32[]{:S(2)}, u32[]{:S(2)}) async-start(f32[128,1,256]{2,1,0:T(1,128)} %reshape.1189), calls=%async_computation.3 | async-start | bytes 262144 | tf_op jit(solution)/shard_map/all_to_all | solution.py:63
  147.4 16.5 %copy-start.4 = (bf16[4,4,1,18,514]{4,1,3,2,0:T(4,128)(2,1)S(1)}, bf16[4,4,1,18,514]{4,1,3,2,0:T(4,128)(2,1)}, u32[]{:S(2)}) copy-start(bf16[4,4,1,18,514]{4,1,3,2,0:T(4,128)(2,1)} %copy-done.3) | copy-start | bytes 888196 | tf_op jit(solution)/shard_map/while
  186.5 16.6 %copy-start.4 = (bf16[4,4,1,18,514]{4,1,3,2,0:T(4,128)(2,1)S(1)}, bf16[4,4,1,18,514]{4,1,3,2,0:T(4,128)(2,1)}, u32[]{:S(2)}) copy-start(bf16[4,4,1,18,514]{4,1,3,2,0:T(4,128)(2,1)} %copy-done.3) | copy-start | bytes 888196 | tf_op jit(solution)/shard_map/while
  264.5 16.5 %copy-start.4 = (bf16[4,4,1,18,514]{4,1,3,2,0:T(4,128)(2,1)S(1)}, bf16[4,4,1,18,514]{4,1,3,2,0:T(4,128)(2,1)}, u32[]{:S(2)}) copy-start(bf16[4,4,1,18,514]{4,1,3,2,0:T(4,128)(2,1)} %copy-done.3) | copy-start | bytes 888196 | tf_op jit(solution)/shard_map/while
  292.0 15.8 %collective-permute-start.2 = (bf16[64,1,1,2048]{3,0,2,1:T(8,128)(2,1)S(1)}, bf16[64,1,1,2048]{3,0,2,1:T(8,128)(2,1)S(1)}, u32[]{:S(2)}, u32[]{:S(2)}) collective-permute-start(bf16[64,1,1,2048]{3,0,2,1:T(8,128)(2,1)S(1)} %get-tuple-element.1375), channel_id=1, source_target_pairs={{0,1},{1,2},{2,3},{3,4},{4,5},{5,6},{6,7},{7,8},{8,9},{9,10},{10,1... | collective-permute-start | bytes 786440 | tf_op jit(solution)/shard_map/ppermute | solution.py:19
  294.6 13.2 %collective-permute-start.3 = (bf16[64,1,1,2048]{3,0,2,1:T(8,128)(2,1)S(1)}, bf16[64,1,1,2048]{3,0,2,1:T(8,128)(2,1)S(1)}, u32[]{:S(2)}, u32[]{:S(2)}) collective-permute-start(bf16[64,1,1,2048]{3,0,2,1:T(8,128)(2,1)S(1)} %get-tuple-element.1376), channel_id=1, source_target_pairs={{1,0},{2,1},{3,2},{4,3},{5,4},{6,5},{7,6},{8,7},{9,8},{10,9},{11,1... | collective-permute-start | bytes 786440 | tf_op jit(solution)/shard_map/ppermute | solution.py:20
  309.9 24.4 %copy-start.61 = (f32[4,64]{1,0:T(4,128)S(1)}, f32[4,64]{1,0:T(4,128)}, u32[]{:S(2)}) copy-start(f32[4,64]{1,0:T(4,128)} %get-tuple-element.1699) | copy-start | bytes 3076
  309.9 24.4 %copy-start.25 = (f32[4,3,3,4,64]{4,3,2,1,0:T(4,128)S(1)}, f32[4,3,3,4,64]{4,3,2,1,0:T(4,128)}, u32[]{:S(2)}) copy-start(f32[4,3,3,4,64]{4,3,2,1,0:T(4,128)} %get-tuple-element.1697) | copy-start | bytes 110596
  310.5 23.8 %copy-start.21 = (f32[4,64,64]{2,1,0:T(8,128)S(1)}, f32[4,64,64]{2,1,0:T(8,128)}, u32[]{:S(2)}) copy-start(f32[4,64,64]{2,1,0:T(8,128)} %get-tuple-element.1698) | copy-start | bytes 196612
  320.9 111.7 %all-to-all-start = ((f32[128,1,256]{2,1,0:T(1,128)}), f32[128,1,256]{2,1,0:T(1,128)S(1)}, u32[]{:S(2)}, u32[]{:S(2)}) async-start(f32[128,1,256]{2,1,0:T(1,128)} %reshape.1183), calls=%async_computation | async-start | bytes 262144 | tf_op jit(solution)/shard_map/all_to_all | solution.py:63
  453.2 21.4 %all-to-all-start.1 = ((f32[128,1,256]{2,1,0:T(1,128)}), f32[128,1,256]{2,1,0:T(1,128)S(1)}, u32[]{:S(2)}, u32[]{:S(2)}) async-start(f32[128,1,256]{2,1,0:T(1,128)} %reshape.1185), calls=%async_computation.1 | async-start | bytes 262144 | tf_op jit(solution)/shard_map/all_to_all | solution.py:63
  (74 other events, 529.0 us)
where the time goes:
time: 496 us; the launch traced here: 487 us
  local copies, waits for them, and re-layouts  164 us (33%)
  blocking collectives  97.6 us (20%)
  other arithmetic  87.3 us (18%)
  starting transfers between devices  66.4 us (13%)
  matrix products  43.4 us (9%)
  waiting for transfers between devices  13.5 us (3%)
  between operations  12.5 us (3%)
    psum x1, blocking collectives, on_device(): lax.psum((conv_total, mixing_total, flux_total), ('rep', 'sp'))  97.6 us
    scatter-add x28, local copies, waits for them, and re-layouts, closure_backward(): piece_cot.at[:, :, row_tap:row_tap + rows, col_tap:col_tap + cols].add(term)  76.6 us
    all_to_all x4, starting transfers between devices, relayout(): moved = lax.all_to_all(field, 'sp', split_axis=2, concat_axis=1, tiled=True)  51.5 us
    unnamed x4, other arithmetic  37.3 us
    unnamed x119, local copies, waits for them, and re-layouts  13.9 us
    all_to_all x4, waiting for transfers between devices, relayout(): moved = lax.all_to_all(field, 'sp', split_axis=2, concat_axis=1, tiled=True)  13.5 us
    another operation x15, other arithmetic  12.7 us
    dot_general x4, matrix products, closure_backward(): jnp.einsum('orxy,prxy->op', first_act, pre_second_cot, preferred_element_...  12.4 us
  transfers between devices with their start and end apart: 8, of which 3 were waited for; matrix products, arithmetic and copies ran while one was open for 11% of the time, Pallas kernels for 0%

commit v1 on v0

--- a/solution.py
+++ b/solution.py
@@ -1,3 +1,4 @@
+import functools
 from functools import partial
 import math
 import jax
@@ -7,6 +8,13 @@
 
 STEPS = 1
 time_step = 0.5
+
+
+def _fit_sheet(body, axis_tag, row_axis):
+    return lax.psum(lax.psum(body, axis_tag), row_axis)
+
+
+_number_rails = functools.partial(_fit_sheet, axis_tag="sp", row_axis="rep")
 
 
 def extended(array, sides, width):
@@ -239,7 +247,7 @@
         inner = inner.at[:, :, -1].add(rim_terms(rims[:, :, 3], conv_weight, 0, side))
         feature_cot = inner.astype(jnp.bfloat16)
         grad = source_grad + feature_cot[0] + 2.0 * height * feature_cot[1]
-    conv_sum, mixing_sum, flux_sum = lax.psum((conv_total, mixing_total, flux_total), ("rep", "sp"))
+    conv_sum, mixing_sum, flux_sum = _number_rails((conv_total, mixing_total, flux_total))
     scale = 1.0 / math.sqrt(lax.axis_size("rep") * film_start.shape[0] * side * side)
     return (final_film, grad, conv_sum * scale, mixing_sum * scale, flux_sum * scale)
 

time: 496 us -> 1140 us (2.30)
  the two profiles are of different devices: /device:TPU:2 before, /device:TPU:1 now
where the time goes in v1:
time: 1140 us; the launch traced here: 1130 us
  blocking collectives  748 us (66%)
  local copies, waits for them, and re-layouts  164 us (14%)
  other arithmetic  87.5 us (8%)
  starting transfers between devices  63.6 us (6%)
  matrix products  42.1 us (4%)
  between operations  12.4 us (1%)
  waiting for transfers between devices  12.1 us (1%)
    psum x2, blocking collectives, _fit_sheet(): return lax.psum(lax.psum(body, axis_tag), row_axis)  748 us
    scatter-add x28, local copies, waits for them, and re-layouts, closure_backward(): piece_cot.at[:, :, row_tap:row_tap + rows, col_tap:col_tap + cols].add(term)  76.6 us
    all_to_all x4, starting transfers between devices, relayout(): moved = lax.all_to_all(field, 'sp', split_axis=2, concat_axis=1, tiled=True)  54.8 us
    unnamed x4, other arithmetic  37.6 us
  transfers between devices with their start and end apart: 8, of which 3 were waited for; matrix products, arithmetic and copies ran while one was open for 5% of the time, Pallas kernels for 0%

profile of v1, /device:TPU:1, one launch (start us, length us, event | category | flops | bytes accessed | tf_op | source)
XLA Modules:
  0.0 1132.3 jit_solution(17907450745668953384)
XLA Ops:
  30.6 9.4 reduce.65
  41.1 20.4 %all-to-all-start.2 = ((f32[128,1,256]{2,1,0:T(1,128)}), f32[128,1,256]{2,1,0:T(1,128)S(1)}, u32[]{:S(2)}, u32[]{:S(2)}) async-start(f32[128,1,256]{2,1,0:T(1,128)} %reshape.1187), calls=%async_computation.2 | async-start | bytes 262144 | tf_op jit(solution)/shard_map/all_to_all | solution.py:71
  82.9 9.4 reduce.67
  93.4 12.9 %all-to-all-start.3 = ((f32[128,1,256]{2,1,0:T(1,128)}), f32[128,1,256]{2,1,0:T(1,128)S(1)}, u32[]{:S(2)}, u32[]{:S(2)}) async-start(f32[128,1,256]{2,1,0:T(1,128)} %reshape.1189), calls=%async_computation.3 | async-start | bytes 262144 | tf_op jit(solution)/shard_map/all_to_all | solution.py:71
  106.4 7.4 while.44
  124.2 156.4 %while.45 = (s32[]{:T(128)}, f32[4,4,1,18,514]{4,1,3,2,0:T(4,128)}, f32[4,3,3,4,64]{4,3,2,1,0:T(4,128)}, f32[4,64,64]{2,1,0:T(8,128)}, f32[4,64]{1,0:T(4,128)}, ...) while((s32[]{:T(128)}, f32[4,4,1,18,514]{4,1,3,2,0:T(4,128)}, ...), condition=%wide.region_90.93_spmd, body=%wide.region_88.92_spmd.sunk | while | flops 327188544 | bytes 51537856 | solution.py:235
  140.8 4.0 scatter-add.90
  146.8 4.1 scatter-add.91
  179.8 4.0 scatter-add.90
  185.8 4.1 scatter-add.91
  218.9 4.0 scatter-add.90
  224.9 4.1 scatter-add.91
  257.9 4.0 scatter-add.90
  263.9 4.1 scatter-add.91
  280.5 4.8 copy.228
  286.0 5.4 fusion.141
  300.1 4.3 copy.231
  307.7 9.4 reduce.69
  318.2 15.1 %all-to-all-start = ((f32[128,1,256]{2,1,0:T(1,128)}), f32[128,1,256]{2,1,0:T(1,128)S(1)}, u32[]{:S(2)}, u32[]{:S(2)}) async-start(f32[128,1,256]{2,1,0:T(1,128)} %reshape.1183), calls=%async_computation | async-start | bytes 262144 | tf_op jit(solution)/shard_map/all_to_all | solution.py:71
  333.4 616.0 %all-reduce.4 = (f32[3,3,4,64]{3,2,1,0:T(4,128)S(1)}, f32[64,64]{1,0:T(8,128)S(1)}, f32[64]{0:T(128)S(1)}) all-reduce(f32[3,3,4,64]{3,2,1,0:T(4,128)S(1)} %reduce_sum.27, f32[64,64]{1,0:T(8,128)S(1)} %reduce_sum.28, f32[64]{0:T(128)S(1)} %reduce_sum.29), channel_id=1, replica_groups=mesh['rep'=4,'sp'=128] {'sp'}, use_global_device_ids=true, to_apply=%region_93.96 | all-reduce | flops 6464 | bytes 51712 | tf_op jit(solution)/shard_map/psum | solution.py:14
  949.4 132.0 %all-reduce.5 = (f32[3,3,4,64]{3,2,1,0:T(4,128)S(1)}, f32[64,64]{1,0:T(8,128)S(1)}, f32[64]{0:T(128)S(1)}) all-reduce(f32[3,3,4,64]{3,2,1,0:T(4,128)S(1)} %get-tuple-element.1340, f32[64,64]{1,0:T(8,128)S(1)} %get-tuple-element.1341, f32[64]{0:T(128)S(1)} %get-tuple-element.1342), channel_id=1, replica_groups=mesh['rep'=4,'sp'=128] {'rep'}, use_global_device_ids=true, to_apply=%region_94.97 | all-reduce | flops 6464 | bytes 51712 | tf_op jit(solution)/shard_map/psum | solution.py:14
  1092.4 9.4 reduce.71
  1102.8 6.4 all-to-all-start.1
  1111.0 9.5 all-to-all-done.1
  (548 shorter events, 229.3 us)
Async XLA Ops:
  0.6 23.3 %copy-start.22 = (f32[1,16,2048]{2,1,0:T(8,128)S(1)}, f32[1,16,2048]{2,1,0:T(8,128)}, u32[]{:S(2)}) copy-start(f32[1,16,2048]{2,1,0:T(8,128)} %param.117) | copy-start | bytes 393220
  1.7 23.1 %copy-start.20 = (f32[4,128,128]{2,1,0:T(8,128)S(1)}, f32[4,128,128]{2,1,0:T(8,128)}, u32[]{:S(2)}) copy-start(f32[4,128,128]{2,1,0:T(8,128)} %param.113) | copy-start | bytes 786436
  3.0 67.8 %collective-permute-start = (bf16[4,1,1,2048]{3,2,1,0:T(2,128)(2,1)S(1)}, bf16[4,1,1,2048]{3,2,1,0:T(2,128)(2,1)S(1)}, u32[]{:S(2)}, u32[]{:S(2)}) collective-permute-start(bf16[4,1,1,2048]{3,2,1,0:T(2,128)(2,1)S(1)} %get-tuple-element.1391), channel_id=1, source_target_pairs={{0,1},{1,2},{2,3},{3,4},{4,5},{5,6},{6,7},{7,8},{8,9},{9,10},{10,1... | collective-permute-start | bytes 49160 | tf_op jit(solution)/shard_map/ppermute | solution.py:27
  6.9 63.9 %collective-permute-start.1 = (bf16[4,1,1,2048]{3,2,1,0:T(2,128)(2,1)S(1)}, bf16[4,1,1,2048]{3,2,1,0:T(2,128)(2,1)S(1)}, u32[]{:S(2)}, u32[]{:S(2)}) collective-permute-start(bf16[4,1,1,2048]{3,2,1,0:T(2,128)(2,1)S(1)} %get-tuple-element.1392), channel_id=1, source_target_pairs={{1,0},{2,1},{3,2},{4,3},{5,4},{6,5},{7,6},{8,7},{9,8},{10,9},{11,1... | collective-permute-start | bytes 49160 | tf_op jit(solution)/shard_map/ppermute | solution.py:28
  15.6 65.0 %copy-start.60 = (s32[256]{0:T(256)}, s32[256]{0:T(256)S(1)}, u32[]{:S(2)}) copy-start(s32[256]{0:T(256)S(1)} %get-tuple-element.1423) | copy-start | bytes 3076
  30.6 33.7 %copy-start.62 = (s32[5]{0:T(128)S(1)}, s32[5]{0:T(128)}, u32[]{:S(2)}) copy-start(s32[5]{0:T(128)} %constant.563.clone.1) | copy-start | bytes 64
  30.6 40.0 %copy-start.5 = (bf16[64,64]{1,0:T(8,128)(2,1)S(1)}, bf16[64,64]{1,0:T(8,128)(2,1)}, u32[]{:S(2)}) copy-start(bf16[64,64]{1,0:T(8,128)(2,1)} %param.115) | copy-start | bytes 24580
  41.1 31.7 %all-to-all-start.2 = ((f32[128,1,256]{2,1,0:T(1,128)}), f32[128,1,256]{2,1,0:T(1,128)S(1)}, u32[]{:S(2)}, u32[]{:S(2)}) async-start(f32[128,1,256]{2,1,0:T(1,128)} %reshape.1187), calls=%async_computation.2 | async-start | bytes 262144 | tf_op jit(solution)/shard_map/all_to_all | solution.py:71
  61.5 16.8 %copy-start.32 = (s32[1024]{0:T(1024)}, s32[1024]{0:T(1024)S(1)}, u32[]{:S(2)}) copy-start(s32[1024]{0:T(1024)S(1)} %pad_clamp_fusion) | copy-start | bytes 12292
  82.3 24.0 %copy-start.12 = (bf16[3,3,4,64]{3,2,1,0:T(4,128)(2,1)S(1)}, bf16[3,3,4,64]{3,2,1,0:T(4,128)(2,1)}, u32[]{:S(2)}) copy-start(bf16[3,3,4,64]{3,2,1,0:T(4,128)(2,1)} %param.114) | copy-start | bytes 13828
  82.3 24.0 %copy-start.26 = (bf16[64]{0:T(256)(128)(2,1)S(1)}, bf16[64]{0:T(256)(128)(2,1)}, u32[]{:S(2)}) copy-start(bf16[64]{0:T(256)(128)(2,1)} %param.116) | copy-start | bytes 388
  82.9 23.4 %copy-start.23 = (f32[4,1,16,512]{3,2,1,0:T(8,128)S(1)}, f32[4,1,16,512]{3,2,1,0:T(8,128)}, u32[]{:S(2)}) copy-start(f32[4,1,16,512]{3,2,1,0:T(8,128)} %custom-call.12) | copy-start | bytes 393220
  93.4 24.3 %all-to-all-start.3 = ((f32[128,1,256]{2,1,0:T(1,128)}), f32[128,1,256]{2,1,0:T(1,128)S(1)}, u32[]{:S(2)}, u32[]{:S(2)}) async-start(f32[128,1,256]{2,1,0:T(1,128)} %reshape.1189), calls=%async_computation.3 | async-start | bytes 262144 | tf_op jit(solution)/shard_map/all_to_all | solution.py:71
  185.8 16.6 %copy-start.4 = (bf16[4,4,1,18,514]{4,1,3,2,0:T(4,128)(2,1)S(1)}, bf16[4,4,1,18,514]{4,1,3,2,0:T(4,128)(2,1)}, u32[]{:S(2)}) copy-start(bf16[4,4,1,18,514]{4,1,3,2,0:T(4,128)(2,1)} %copy-done.3) | copy-start | bytes 888196 | tf_op jit(solution)/shard_map/while
  185.8 16.6 %copy-start.14 = (bf16[3,3,4,64]{3,2,1,0:T(4,128)(2,1)S(1)}, bf16[3,3,4,64]{3,2,1,0:T(4,128)(2,1)}, u32[]{:S(2)}) copy-start(bf16[3,3,4,64]{3,2,1,0:T(4,128)(2,1)} %copy-done.13) | copy-start | bytes 13828 | tf_op jit(solution)/shard_map/while
  263.9 16.6 %copy-start.4 = (bf16[4,4,1,18,514]{4,1,3,2,0:T(4,128)(2,1)S(1)}, bf16[4,4,1,18,514]{4,1,3,2,0:T(4,128)(2,1)}, u32[]{:S(2)}) copy-start(bf16[4,4,1,18,514]{4,1,3,2,0:T(4,128)(2,1)} %copy-done.3) | copy-start | bytes 888196 | tf_op jit(solution)/shard_map/while
  263.9 16.6 %copy-start.14 = (bf16[3,3,4,64]{3,2,1,0:T(4,128)(2,1)S(1)}, bf16[3,3,4,64]{3,2,1,0:T(4,128)(2,1)}, u32[]{:S(2)}) copy-start(bf16[3,3,4,64]{3,2,1,0:T(4,128)(2,1)} %copy-done.13) | copy-start | bytes 13828 | tf_op jit(solution)/shard_map/while
  291.5 13.5 %collective-permute-start.2 = (bf16[64,1,1,2048]{3,0,2,1:T(8,128)(2,1)S(1)}, bf16[64,1,1,2048]{3,0,2,1:T(8,128)(2,1)S(1)}, u32[]{:S(2)}, u32[]{:S(2)}) collective-permute-start(bf16[64,1,1,2048]{3,0,2,1:T(8,128)(2,1)S(1)} %get-tuple-element.1378), channel_id=1, source_target_pairs={{0,1},{1,2},{2,3},{3,4},{4,5},{5,6},{6,7},{7,8},{8,9},{9,10},{10,1... | collective-permute-start | bytes 786440 | tf_op jit(solution)/shard_map/ppermute | solution.py:27
  293.7 11.3 collective-permute-start.3
  307.1 26.2 %copy-start.61 = (f32[4,64]{1,0:T(4,128)S(1)}, f32[4,64]{1,0:T(4,128)}, u32[]{:S(2)}) copy-start(f32[4,64]{1,0:T(4,128)} %get-tuple-element.1702) | copy-start | bytes 3076
  307.1 26.2 %copy-start.25 = (f32[4,3,3,4,64]{4,3,2,1,0:T(4,128)S(1)}, f32[4,3,3,4,64]{4,3,2,1,0:T(4,128)}, u32[]{:S(2)}) copy-start(f32[4,3,3,4,64]{4,3,2,1,0:T(4,128)} %get-tuple-element.1700) | copy-start | bytes 110596
  307.7 25.7 %copy-start.21 = (f32[4,64,64]{2,1,0:T(8,128)S(1)}, f32[4,64,64]{2,1,0:T(8,128)}, u32[]{:S(2)}) copy-start(f32[4,64,64]{2,1,0:T(8,128)} %get-tuple-element.1701) | copy-start | bytes 196612
  318.2 763.9 %all-to-all-start = ((f32[128,1,256]{2,1,0:T(1,128)}), f32[128,1,256]{2,1,0:T(1,128)S(1)}, u32[]{:S(2)}, u32[]{:S(2)}) async-start(f32[128,1,256]{2,1,0:T(1,128)} %reshape.1183), calls=%async_computation | async-start | bytes 262144 | tf_op jit(solution)/shard_map/all_to_all | solution.py:71
  1102.8 17.7 %all-to-all-start.1 = ((f32[128,1,256]{2,1,0:T(1,128)}), f32[128,1,256]{2,1,0:T(1,128)S(1)}, u32[]{:S(2)}, u32[]{:S(2)}) async-start(f32[128,1,256]{2,1,0:T(1,128)} %reshape.1185), calls=%async_computation.1 | async-start | bytes 262144 | tf_op jit(solution)/shard_map/all_to_all | solution.py:71
  (74 other events, 518.4 us)
